TPU v7x, 256 devices: a whole 4x4x8 slice. The times are simulated.
256 devices in a mesh: head: 4 (over z_hi, core), inner: 16 (over z_lo, x), outer: 4 (over y).
Axes of the slice: x: 4, y: 4, z: 8 (z_hi: 2, z_lo: 4; z = z_hi * 4 + z_lo), core: 2. Of those that a mesh axis runs over, the one named last changes fastest.
Arguments:
- query_states: bfloat16 [8192, 8192], P('outer', 'inner'), may hold values from -110 to 110
- context_hidden_states: bfloat16 [16384, 8192], P(('inner', 'outer'), 'head'), may hold values from -6 to 6
- key_segments: int32 [128], P(('inner', 'outer')), may hold values from 0 to 6, as said below
- query_segments: int32 [8192], P('outer'), may hold values from 1 to 6, as said below
- w_query: bfloat16 [8192, 4096], P('inner', 'head'), may hold values from -0.1875 to 0.1875
- key_value_weight: bfloat16 [8192, 4, 256], P('head'), may hold values from -0.0625 to 0.0625
- w_output: bfloat16 [4096, 4, 2048], P('head', None, 'inner'), may hold values from -0.09375 to 0.09375
Outputs:
- mixed: bfloat16 [8192, 8192], P('outer', ('head', 'inner'))
Inputs may be any that keep to these rules, and one draw needn't show every extreme that they name: `key_segments`: block 0 is repository code (0) and the last block has segment 6. `query_segments`: the first query token has span 1 and the last has span 6.
All inputs are finite; a program needn't handle non-finite values.
Results may differ from a plain program's by a relative error of at most 0.0173.
The roundings to bfloat16 on the way count: a program that leaves them out, or rounds other values in their place, can miss the bound.
Values may be sent and summed in bfloat16 or wider, within the bound.
A program may use at most 128 MiB of HBM per device.

v0:
```python
import math

import jax
import jax.numpy as jnp
from jax import lax
from jax.sharding import PartitionSpec as P

HEAD_SIZE = 128
KBLK = 128
QWIN = 512


ROPE_BASE = 1000000.0
NEG_FILL = -1e30


def rotate(vectors, positions):
    half = HEAD_SIZE // 2
    freqs = jnp.power(ROPE_BASE, -(jnp.arange(half).astype(jnp.float32) * 2.0 / HEAD_SIZE))
    angles = positions[:, None] * freqs[None, :]
    cosine = jnp.cos(angles)[:, None, :]
    sine = jnp.sin(angles)[:, None, :]
    lower = vectors[..., :half]
    upper = vectors[..., half:]
    return jnp.concatenate([lower * cosine - upper * sine, upper * cosine + lower * sine], axis=-1)


def on_device(
    query_states,
    context_hidden_states,
    key_segments,
    query_segments,
    w_query,
    key_value_weight,
    w_output,
):
    head_count = lax.axis_size("head")
    inner_count = lax.axis_size("inner")
    outer_count = lax.axis_size("outer")
    inner_at = lax.axis_index("inner")
    outer_at = lax.axis_index("outer")
    query_rows = query_states.shape[0] // inner_count
    query_cols = w_query.shape[1]
    local_heads = query_cols // HEAD_SIZE
    groups = key_value_weight.shape[1] // head_count
    head_repeat_count = local_heads // groups
    context_rows = context_hidden_states.shape[0]
    context_len = context_rows * inner_count * outer_count
    scale = 1.0 / math.sqrt(HEAD_SIZE)
    projected_q = lax.psum_scatter(
        jnp.dot(query_states, w_query, preferred_element_type=jnp.float32),
        "inner",
        scatter_dimension=0,
        tiled=True,
    )
    row_first = outer_at * query_states.shape[0] + inner_at * query_rows
    query_pos = (context_len + (row_first + jnp.arange(query_rows)) % QWIN).astype(jnp.float32)
    queries = rotate(projected_q.reshape(query_rows, local_heads, HEAD_SIZE), query_pos).astype(
        jnp.bfloat16
    )
    queries = queries.reshape(query_rows, groups, head_repeat_count, HEAD_SIZE)
    query_tags = lax.dynamic_slice_in_dim(query_segments, inner_at * query_rows, query_rows, 0)
    kv_partial = jnp.dot(
        context_hidden_states,
        key_value_weight.reshape(key_value_weight.shape[0], -1),
        preferred_element_type=jnp.float32,
    )
    kv_partial = kv_partial.reshape(context_rows, key_value_weight.shape[1], 2 * HEAD_SIZE)
    kv_local = lax.psum_scatter(kv_partial, "head", scatter_dimension=1, tiled=True)
    key_first = (inner_at * outer_count + outer_at) * context_rows
    key_pos = (key_first + jnp.arange(context_rows)).astype(jnp.float32)
    keys = (
        rotate(kv_local[:, :, :HEAD_SIZE], key_pos)
        .astype(jnp.bfloat16)
        .reshape(context_rows, groups * HEAD_SIZE)
    )
    values = (
        kv_local[:, :, HEAD_SIZE:].astype(jnp.bfloat16).reshape(context_rows, groups * HEAD_SIZE)
    )
    key_tags = jnp.repeat(key_segments, KBLK)

    def attend_block(state, block_keys, block_values, block_tags):
        running_max, running_sum, accumulated = state
        count = block_keys.shape[0]
        key_mat = block_keys.reshape(count, groups, HEAD_SIZE)
        value_mat = block_values.reshape(count, groups, HEAD_SIZE)
        scores = (
            jnp.einsum("rgph,ngh->rgpn", queries, key_mat, preferred_element_type=jnp.float32)
            * scale
        )
        allowed = (block_tags[None, :] == 0) | (block_tags[None, :] == query_tags[:, None])
        allowed = allowed[:, None, None, :]
        new_max = jnp.maximum(running_max, jnp.max(jnp.where(allowed, scores, NEG_FILL), axis=-1))
        weights = jnp.where(allowed, jnp.exp(scores - new_max[..., None]), 0.0)
        factor = jnp.exp(running_max - new_max)
        running_sum = running_sum * factor + jnp.sum(weights, axis=-1)
        update = jnp.einsum(
            "rgpn,ngh->rgph",
            weights.astype(jnp.bfloat16),
            value_mat,
            preferred_element_type=jnp.float32,
        )
        accumulated = accumulated * factor[..., None] + update
        return (new_max, running_sum, accumulated)

    start_state = (
        jnp.full((query_rows, groups, head_repeat_count), NEG_FILL, jnp.float32),
        jnp.zeros((query_rows, groups, head_repeat_count), jnp.float32),
        jnp.zeros((query_rows, groups, head_repeat_count, HEAD_SIZE), jnp.float32),
    )
    block_keys = lax.all_gather(keys, ("inner", "outer"), axis=0, tiled=True)
    block_values = lax.all_gather(values, ("inner", "outer"), axis=0, tiled=True)
    block_tags = lax.all_gather(key_tags, ("inner", "outer"), axis=0, tiled=True)
    count = block_keys.shape[0]
    width = math.gcd(count, 1024)

    def scan_step(carried, sliced):
        return (attend_block(carried, sliced[0], sliced[1], sliced[2]), None)

    stacked = (
        block_keys.reshape(count // width, width, -1),
        block_values.reshape(count // width, width, -1),
        block_tags.reshape(count // width, width),
    )
    finished, unused = lax.scan(scan_step, start_state, stacked)
    attended = (
        (finished[2] / finished[1][..., None]).reshape(query_rows, query_cols).astype(jnp.bfloat16)
    )
    output_flat = w_output.reshape(w_output.shape[0], -1)
    terms = jnp.dot(
        lax.all_gather(attended, "inner", axis=0, tiled=True),
        output_flat,
        preferred_element_type=jnp.float32,
    )
    terms = terms.reshape(terms.shape[0], head_count, -1)
    mixed = lax.psum_scatter(
        terms.astype(jnp.bfloat16), "head", scatter_dimension=1, tiled=True
    ).astype(jnp.float32)
    return mixed.reshape(terms.shape[0], -1).astype(jnp.bfloat16)


def solution(mesh):
    in_specs = (
        P("outer", "inner"),
        P(("inner", "outer"), "head"),
        P(("inner", "outer")),
        P("outer"),
        P("inner", "head"),
        P("head", None, None),
        P("head", None, "inner"),
    )
    out_specs = P("outer", ("head", "inner"))
    return jax.shard_map(
        on_device, mesh=mesh, in_specs=in_specs, out_specs=out_specs, check_vma=False
    )
```

profile of v0, /device:TPU:1, one launch (start us, length us, event | category | flops | bytes accessed | tf_op | source)
XLA Modules:
  0.0 1172.7 jit_solution(10773473520648076739)
XLA Ops:
  6.5 5.4 copy.27
  11.9 6.6 copy.16
  18.5 4.5 fusion.31
  23.1 6.8 fusion.49
  30.0 42.0 %reduce-scatter.4.cloned.1.call-done = f32[256,1,256]{2,0,1:T(8,128)} async-done(((f32[256,4,256]{2,0,1:T(8,128)}), f32[256,1,256]{2,0,1:T(8,128)}) %reduce-scatter.4.cloned.1.call-update) | async-done | bytes 262160 | tf_op jit(solution)/shard_map/reduce_scatter | solution.py:69
  72.0 1.6 fusion.44
  74.4 1.5 slice.42
  76.1 156.3 %all-gather.1 = s32[64,1,256]{2,1,0:T(1,128)S(1)} all-gather(s32[1,1,256]{2,1,0:T(1,128)S(1)} %bitcast.139), channel_id=1, replica_groups=mesh['head'=4,'inner'=16,'outer'=4] {'inner','outer'}, dimensions={0}, use_global_device_ids=true | all-gather | bytes 66560 | tf_op jit(solution)/shard_map/all_gather | solution.py:113
  233.7 1.1 copy.28
  235.4 247.3 %all-gather.6.cloned.1.call-done = bf16[16384,128]{1,0:T(8,128)(2,1)} async-done(((bf16[256,128]{1,0:T(8,128)(2,1)}), bf16[16384,128]{1,0:T(8,128)(2,1)}) %all-gather.6.cloned.1.call-update) | async-done | bytes 4194320 | tf_op jit(solution)/shard_map/all_gather | solution.py:111
  482.7 352.8 %all-gather.10.cloned.1.call-done = bf16[16384,1,128]{2,0,1:T(8,128)(2,1)} async-done(((bf16[256,1,128]{2,0,1:T(8,128)(2,1)}), bf16[16384,1,128]{2,0,1:T(8,128)(2,1)}) %all-gather.10.cloned.1.call-update) | async-done | bytes 4194320 | tf_op jit(solution)/shard_map/all_gather | solution.py:112
  835.5 135.5 %while.15 = (s32[]{:T(128)}, f32[128,1,8]{0,2,1:T(8,128)S(1)}, f32[128,1,8]{0,2,1:T(8,128)S(1)}, f32[128,1,8,128]{0,3,2,1:T(8,128)S(1)}, s32[16,1024]{1,0:T(8,12...) while((s32[]{:T(128)}, f32[128,1,8]{0,2,1:T(8,128)S(1)}, ...), condition=%wide.region_5.6_spmd.clone, body=%wide.region_2.5_spmd.clone.sunk | while | flops 549067776 | bytes 31800984 | solution.py:125
  835.9 3.7 fusion.62
  839.6 3.4 fusion.65
  843.1 0.9 fusion.64
  844.4 3.7 fusion.62
  848.1 3.4 fusion.65
  851.6 0.9 fusion.64
  852.9 3.7 fusion.62
  856.5 3.4 fusion.65
  860.1 0.9 fusion.64
  861.3 3.7 fusion.62
  865.0 3.4 fusion.65
  868.5 0.9 fusion.64
  869.8 3.7 fusion.62
  873.5 3.4 fusion.65
  877.0 0.9 fusion.64
  878.3 3.7 fusion.62
  882.0 3.4 fusion.65
  885.5 0.9 fusion.64
  886.7 3.7 fusion.62
  890.4 3.4 fusion.65
  893.9 0.9 fusion.64
  895.2 3.7 fusion.62
  898.9 3.4 fusion.65
  902.4 0.9 fusion.64
  903.7 3.7 fusion.62
  907.4 3.4 fusion.65
  910.9 0.9 fusion.64
  912.2 3.7 fusion.62
  915.8 3.4 fusion.65
  919.4 0.9 fusion.64
  920.6 3.7 fusion.62
  924.3 3.4 fusion.65
  927.8 0.9 fusion.64
  929.1 3.7 fusion.62
  932.8 3.4 fusion.65
  936.3 0.9 fusion.64
  937.6 3.7 fusion.62
  941.3 3.4 fusion.65
  944.8 0.9 fusion.64
  946.1 3.7 fusion.62
  949.7 3.4 fusion.65
  953.2 0.9 fusion.64
  954.5 3.7 fusion.62
  958.2 3.4 fusion.65
  961.7 0.9 fusion.64
  963.0 3.7 fusion.62
  966.7 3.4 fusion.65
  972.3 1.4 copy.43
  973.7 1.3 copy.21
  975.0 119.7 %all-gather.8.cloned.1.call-done = bf16[2048,1024]{1,0:T(8,128)(2,1)} async-done(((bf16[128,1024]{1,0:T(8,128)(2,1)}), bf16[2048,1024]{1,0:T(8,128)(2,1)}) %all-gather.8.cloned.1.call-update) | async-done | bytes 4194320 | tf_op jit(solution)/shard_map/all_gather | solution.py:131
  1094.7 6.2 fusion.28
  1100.9 65.0 %reduce-scatter.8.cloned.1.call-done = bf16[2048,1,128]{2,0,1:T(8,128)(2,1)} async-done(((bf16[2048,4,128]{2,0,1:T(8,128)(2,1)}), bf16[2048,1,128]{2,0,1:T(8,128)(2,1)}) %reduce-scatter.8.cloned.1.call-update) | async-done | bytes 524304 | tf_op jit(solution)/shard_map/reduce_scatter | solution.py:136
  (149 shorter events, 12.4 us)
Async XLA Ops:
  6.5 16.5 %copy-start = (bf16[2048,512]{1,0:T(8,128)(2,1)S(1)}, bf16[2048,512]{1,0:T(8,128)(2,1)}, u32[]{:S(2)}) copy-start(bf16[2048,512]{1,0:T(8,128)(2,1)} %param.9) | copy-start | bytes 6291460
  6.5 65.5 %reduce-scatter.4.cloned.1.call-start = ((), (), s32[]{:S(2)}) async-start(), calls=%async_computation.3 | async-start | bytes 1310720 | tf_op jit(solution)/shard_map/reduce_scatter | solution.py:69
  11.9 6.6 copy-start.2
  23.0 210.7 %reduce-scatter.6.cloned.1.call-start = ((), (), s32[]{:S(2)}) async-start(), calls=%async_computation.5 | async-start | bytes 8912896 | tf_op jit(solution)/shard_map/reduce_scatter | solution.py:50
  29.9 46.1 %copy-start.3 = (s32[2]{0:T(128)S(1)}, s32[2]{0:T(128)}, u32[]{:S(2)}) copy-start(s32[2]{0:T(128)} %param.11) | copy-start | bytes 28
  29.9 452.8 %all-gather.6.cloned.1.call-start = ((), (), s32[]{:S(2)}) async-start(), calls=%async_computation.4 | async-start | bytes 4259840 | tf_op jit(solution)/shard_map/all_gather | solution.py:111
  74.3 761.2 %all-gather.10.cloned.1.call-start = ((), (), s32[]{:S(2)}) async-start(), calls=%async_computation.8 | async-start | bytes 4259840 | tf_op jit(solution)/shard_map/all_gather | solution.py:112
  75.9 1018.8 %all-gather.8.cloned.1.call-start = ((), (), s32[]{:S(2)}) async-start(), calls=%async_computation.6 | async-start | bytes 4456448 | tf_op jit(solution)/shard_map/all_gather | solution.py:131
  839.6 3.5 copy-start.1
  848.1 3.5 copy-start.1
  856.5 3.5 copy-start.1
  865.0 3.5 copy-start.1
  873.5 3.5 copy-start.1
  881.9 3.5 copy-start.1
  890.4 3.5 copy-start.1
  898.9 3.5 copy-start.1
  907.4 3.5 copy-start.1
  915.8 3.5 copy-start.1
  924.3 3.5 copy-start.1
  932.8 3.5 copy-start.1
  941.2 3.5 copy-start.1
  949.7 3.5 copy-start.1
  958.2 3.5 copy-start.1
  966.7 3.5 copy-start.1
  972.0 193.8 %reduce-scatter.8.cloned.1.call-start = ((), (), s32[]{:S(2)}) async-start(), calls=%async_computation.7 | async-start | bytes 2621440 | tf_op jit(solution)/shard_map/reduce_scatter | solution.py:136
Sparse Core Ops, SparseCore 0:
  23.1 48.8 reduce-scatter.3
  74.6 95.7 reduce-scatter.5
  172.2 310.5 all-gather.5
  484.4 351.1 all-gather.9
  972.1 122.4 all-gather.7
  1101.0 64.7 reduce-scatter.7
where the time goes:
time: 1170 us
  waiting for transfers between devices  827 us (71%)
  blocking collectives  156 us (13%)
  matrix products  131 us (11%)
  other arithmetic  23.2 us (2%)
  local copies, waits for them, and re-layouts  20.5 us (2%)
  between operations  13.6 us (1%)
    all_gather x1, waiting for transfers between devices, on_device(): lax.all_gather(values, ('inner', 'outer'), axis=0, tiled=True)  353 us
    all_gather x1, waiting for transfers between devices, on_device(): block_keys = lax.all_gather(keys, ('inner', 'outer'), axis=0, tiled=True)  247 us
    all_gather x1, blocking collectives, on_device(): lax.all_gather(key_tags, ('inner', 'outer'), axis=0, tiled=True)  156 us
    all_gather x1, waiting for transfers between devices, on_device(): lax.all_gather(attended, 'inner', axis=0, tiled=True)  120 us
    reduce_scatter x1, waiting for transfers between devices, on_device(): lax.psum_scatter(terms.astype(jnp.bfloat16), 'head', scatter_dimension=1,...  65 us
    dot_general x16, matrix products, attend_block(): jnp.einsum('rgph,ngh->rgpn', queries, key_mat, preferred_element_type=jnp...  58.6 us
    dot_general x16, matrix products, attend_block(): jnp.einsum('rgpn,ngh->rgph', weights.astype(jnp.bfloat16), value_mat, pre...  54.9 us
    reduce_scatter x1, waiting for transfers between devices, on_device(): lax.psum_scatter(kv_partial, 'head', scatter_dimension=1, tiled=True)  42 us
  transfers between devices with their start and end apart: 6, of which 5 were waited for; matrix products, arithmetic and copies ran while one was open for 1% of the time, Pallas kernels for 0%

commit v1 on v0

v1 whole, which is shorter than its diff:
```python
import math

import jax
import jax.numpy as jnp
from jax import lax
from jax.experimental import pallas as pl
from jax.experimental.pallas import tpu as pltpu
from jax.sharding import PartitionSpec as P

HEAD_SIZE = 128
KBLK = 128
QWIN = 512
ROPE_BASE = 1000000.0
PENALTY = -1e30
SCALE2 = math.log2(math.e) / math.sqrt(HEAD_SIZE)


def rotate(vectors, positions):
    half = HEAD_SIZE // 2
    freqs = jnp.power(ROPE_BASE, -(jnp.arange(half).astype(jnp.float32) * 2.0 / HEAD_SIZE))
    angles = positions[:, None] * freqs[None, :]
    cosine = jnp.cos(angles)[:, None, :]
    sine = jnp.sin(angles)[:, None, :]
    lower = vectors[..., :half]
    upper = vectors[..., half:]
    return jnp.concatenate([lower * cosine - upper * sine, upper * cosine + lower * sine], axis=-1)


def attention_kernel(heads, tile, chunk, q_ref, hot_ref, ka_ref, va_ref, o_ref, lse_ref, s_ref, m_ref):
    tokens = q_ref.shape[0]
    keys = ka_ref.shape[0]
    halves = tokens // tile
    steps = heads * halves
    chunks = keys // chunk

    def rows_of(t):
        return pl.ds(pl.multiple_of(lax.rem(t, halves) * tile, tile), tile)

    def cols_of(t):
        return pl.ds(pl.multiple_of(lax.div(t, halves) * HEAD_SIZE, HEAD_SIZE), HEAD_SIZE)

    def score(t, slot, c):
        qa = jnp.concatenate([q_ref[rows_of(t), cols_of(t)], hot_ref[rows_of(t), :]], axis=-1)
        s = lax.dot_general(
            qa, ka_ref[c * chunk : (c + 1) * chunk, :],
            (((1,), (1,)), ((), ())), preferred_element_type=jnp.float32,
        )
        s_ref[slot, :, c * chunk : (c + 1) * chunk] = s
        best = s[:, :HEAD_SIZE]
        for j in range(1, chunk // HEAD_SIZE):
            best = jnp.maximum(best, s[:, j * HEAD_SIZE : (j + 1) * HEAD_SIZE])
        return best

    def top_of(bests):
        best = bests[0]
        for b in bests[1:]:
            best = jnp.maximum(best, b)
        return jnp.broadcast_to(jnp.max(best, axis=-1, keepdims=True) * SCALE2, (tile, HEAD_SIZE))

    m_ref[0] = top_of([score(0, 0, c) for c in range(chunks)])
    lane = lax.broadcasted_iota(jnp.int32, (tile, HEAD_SIZE), 1)

    def body(t, carry):
        slot = lax.rem(t, 2)
        nxt = jnp.minimum(t + 1, steps - 1)
        m = m_ref[slot]
        acc = jnp.zeros((tile, 2 * HEAD_SIZE), jnp.float32)
        bests = []
        mw = jnp.concatenate([m] * (chunk // HEAD_SIZE), axis=-1)
        for c in range(chunks):
            p = jnp.exp2(s_ref[slot, :, c * chunk : (c + 1) * chunk] * SCALE2 - mw)
            bests.append(score(nxt, 1 - slot, c))
            acc += jnp.dot(p.astype(jnp.bfloat16), va_ref[c * chunk : (c + 1) * chunk, :], preferred_element_type=jnp.float32)
        m_ref[1 - slot] = top_of(bests)
        total = acc[:, HEAD_SIZE:]
        o_ref[rows_of(t), cols_of(t)] = (acc[:, :HEAD_SIZE] / total).astype(jnp.bfloat16)
        lse = m + jnp.log2(total)
        old = lse_ref[rows_of(t), :]
        lse_ref[rows_of(t), :] = jnp.where(lane == lax.div(t, halves), lse, old)
        return carry

    lse_ref[...] = jnp.zeros_like(lse_ref)
    lax.fori_loop(0, steps, body, 0)


def attention(q, hot, ka, va, heads, tile=256, chunk=512):
    tokens = q.shape[0]
    keys = ka.shape[0]
    return pl.pallas_call(
        lambda *refs: attention_kernel(heads, tile, chunk, *refs),
        out_shape=(
            jax.ShapeDtypeStruct(q.shape, jnp.bfloat16),
            jax.ShapeDtypeStruct((tokens, HEAD_SIZE), jnp.float32),
        ),
        in_specs=[pl.BlockSpec(memory_space=pltpu.VMEM)] * 4,
        out_specs=(pl.BlockSpec(memory_space=pltpu.VMEM),) * 2,
        scratch_shapes=[
            pltpu.VMEM((2, tile, keys), jnp.float32),
            pltpu.VMEM((2, tile, HEAD_SIZE), jnp.float32),
        ],
        compiler_params=pltpu.CompilerParams(vmem_limit_bytes=48 * 1024 * 1024),
        name="attention",
    )(q, hot, ka, va)


def penalties(tags, rows):
    lane = jnp.arange(HEAD_SIZE, dtype=jnp.int32)
    row = jnp.where((tags[:, None] == 0) | (tags[:, None] == lane[None, :]), 0.0, PENALTY)
    return jnp.repeat(row.astype(jnp.bfloat16), rows, axis=0)


def on_device(
    query_states,
    context_hidden_states,
    key_segments,
    query_segments,
    w_query,
    key_value_weight,
    w_output,
):
    head_count = lax.axis_size("head")
    inner_count = lax.axis_size("inner")
    outer_count = lax.axis_size("outer")
    inner_at = lax.axis_index("inner")
    outer_at = lax.axis_index("outer")
    query_rows = query_states.shape[0] // inner_count
    query_cols = w_query.shape[1]
    heads = query_cols // HEAD_SIZE
    context_rows = context_hidden_states.shape[0]
    context_len = context_rows * inner_count * outer_count
    projected_q = lax.psum_scatter(
        jnp.dot(query_states, w_query, preferred_element_type=jnp.float32),
        "inner",
        scatter_dimension=0,
        tiled=True,
    )
    row_first = outer_at * query_states.shape[0] + inner_at * query_rows
    query_pos = (context_len + (row_first + jnp.arange(query_rows)) % QWIN).astype(jnp.float32)
    queries = rotate(projected_q.reshape(query_rows, heads, HEAD_SIZE), query_pos).astype(
        jnp.bfloat16
    )
    queries = queries.reshape(query_rows, query_cols)
    query_tags = lax.dynamic_slice_in_dim(query_segments, inner_at * query_rows, query_rows, 0)
    hot = (query_tags[:, None] == jnp.arange(HEAD_SIZE)[None, :]).astype(jnp.bfloat16)
    kv_partial = jnp.dot(
        context_hidden_states,
        key_value_weight.reshape(key_value_weight.shape[0], -1),
        preferred_element_type=jnp.float32,
    )
    kv_partial = kv_partial.reshape(context_rows, key_value_weight.shape[1], 2 * HEAD_SIZE)
    kv_local = lax.psum_scatter(kv_partial, "head", scatter_dimension=1, tiled=True)
    key_first = (inner_at * outer_count + outer_at) * context_rows
    key_pos = (key_first + jnp.arange(context_rows)).astype(jnp.float32)
    keys = rotate(kv_local[:, :, :HEAD_SIZE], key_pos).astype(jnp.bfloat16)[:, 0]
    values = kv_local[:, 0, HEAD_SIZE:].astype(jnp.bfloat16)
    packed = jnp.concatenate([keys, values, penalties(key_segments, KBLK)], axis=-1)
    gathered = lax.all_gather(packed, "inner", axis=0, tiled=True)
    ka = jnp.concatenate([gathered[:, :HEAD_SIZE], gathered[:, 2 * HEAD_SIZE :]], axis=-1)
    va = jnp.concatenate(
        [gathered[:, HEAD_SIZE : 2 * HEAD_SIZE], jnp.ones((ka.shape[0], HEAD_SIZE), jnp.bfloat16)],
        axis=-1,
    )
    qall = lax.all_gather(jnp.concatenate([queries, hot], axis=-1), "outer", axis=0, tiled=True)
    part, lse = attention(qall[:, :query_cols], qall[:, query_cols:], ka, va, heads)
    lse = lse[:, :heads].reshape(outer_count, query_rows, heads)
    part = lax.all_to_all(
        part.reshape(outer_count, query_rows, query_cols), "outer", 0, 0, tiled=True
    )
    lse = lax.all_to_all(lse, "outer", 0, 0, tiled=True)
    weight = jnp.exp2(lse - jnp.max(lse, axis=0, keepdims=True))
    weight = weight / jnp.sum(weight, axis=0, keepdims=True)
    attended = jnp.sum(
        part.reshape(outer_count, query_rows, heads, HEAD_SIZE).astype(jnp.float32)
        * weight[..., None],
        axis=0,
    )
    attended = attended.reshape(query_rows, query_cols).astype(jnp.bfloat16)
    output_flat = w_output.reshape(w_output.shape[0], -1)
    terms = jnp.dot(
        lax.all_gather(attended, "inner", axis=0, tiled=True),
        output_flat,
        preferred_element_type=jnp.float32,
    )
    terms = terms.reshape(terms.shape[0], head_count, -1)
    mixed = lax.psum_scatter(
        terms.astype(jnp.bfloat16), "head", scatter_dimension=1, tiled=True
    ).astype(jnp.float32)
    return mixed.reshape(terms.shape[0], -1).astype(jnp.bfloat16)


def solution(mesh):
    in_specs = (
        P("outer", "inner"),
        P(("inner", "outer"), "head"),
        P(("inner", "outer")),
        P("outer"),
        P("inner", "head"),
        P("head", None, None),
        P("head", None, "inner"),
    )
    out_specs = P("outer", ("head", "inner"))
    return jax.shard_map(
        on_device, mesh=mesh, in_specs=in_specs, out_specs=out_specs, check_vma=False
    )
```

time: 1170 us -> 529 us (0.45)
  waiting for transfers between devices: 827 us -> 395 us
  blocking collectives: 156 us -> 7.51 us
  matrix products: 131 us -> 17.5 us
  Pallas kernels: 0 us -> 54.1 us
  other arithmetic: 23.2 us -> 8.23 us
    all_gather x2, waiting for transfers between devices: 600 us -> 109 us  [the longest x1 80 us: on_device(): gathered = lax.all_gather(packed, 'inner', axis=0, tiled=True)]
    all_gather x1 -> x0, blocking collectives: 156 us -> none  [on_device(): lax.all_gather(key_tags, ('inner', 'outer'), axis=0, tiled=True)]
    dot_general x32 -> x0, matrix products: 114 us -> none  [the longest x16 58.6 us: attend_block(): jnp.einsum('rgph,ngh->rgpn', queries, key_mat, preferred_element_type=jnp...]
    reduce_scatter x1, waiting for transfers between devices: 0.02 us -> 93.8 us  [on_device(): lax.psum_scatter(jnp.dot(query_states, w_query, preferred_element_type=jn...]
    pallas_call x0 -> x1, Pallas kernels: none -> 54.1 us  [attention(): pl.pallas_call(lambda *refs: attention_kernel(heads, tile, chunk, *refs),...]
    all_gather x1, waiting for transfers between devices: 120 us -> 79.4 us  [on_device(): lax.all_gather(attended, 'inner', axis=0, tiled=True)]
  transfers between devices with their start and end apart: 6 -> 7, of which waited for: 5 -> 7; matrix products, arithmetic and copies ran while one was open for 1% -> 5% of each run, Pallas kernels for 0% -> 0%
where the time goes in v1:
time: 529 us; the launch traced here: 528 us
  waiting for transfers between devices  395 us (75%)
  Pallas kernels  54.1 us (10%)
  local copies, waits for them, and re-layouts  28.9 us (5%)
  matrix products  17.5 us (3%)
  between operations  13.6 us (3%)
  other arithmetic  8.23 us (2%)
  blocking collectives  7.51 us (1%)
    reduce_scatter x1, waiting for transfers between devices, on_device(): lax.psum_scatter(jnp.dot(query_states, w_query, preferred_element_type=jn...  93.8 us
    all_gather x1, waiting for transfers between devices, on_device(): gathered = lax.all_gather(packed, 'inner', axis=0, tiled=True)  80 us
    all_gather x1, waiting for transfers between devices, on_device(): lax.all_gather(attended, 'inner', axis=0, tiled=True)  79.4 us
    reduce_scatter x1, waiting for transfers between devices, on_device(): lax.psum_scatter(terms.astype(jnp.bfloat16), 'head', scatter_dimension=1,...  65 us
    pallas_call x1, Pallas kernels, attention(): pl.pallas_call(lambda *refs: attention_kernel(heads, tile, chunk, *refs),...  54.1 us
    reduce_scatter x1, waiting for transfers between devices, on_device(): lax.psum_scatter(kv_partial, 'head', scatter_dimension=1, tiled=True)  41.4 us
    all_gather x1, waiting for transfers between devices, on_device(): lax.all_gather(jnp.concatenate([queries, hot], axis=-1), 'outer', axis=0,...  29.1 us
  transfers between devices with their start and end apart: 7, of which 7 were waited for; matrix products, arithmetic and copies ran while one was open for 5% of the time, Pallas kernels for 0%

profile of v1, /device:TPU:1, one launch (start us, length us, event | category | flops | bytes accessed | tf_op | source)
XLA Modules:
  0.0 528.3 jit_solution(13513612949327299356)
XLA Ops:
  6.5 0.0 copy-start
  6.5 0.0 reduce-scatter.6.cloned.1.call-start
  6.5 5.3 %copy.16 = bf16[256,8,4,256]{3,1,2,0:T(8,128)(2,1)} copy(bf16[256,8,4,256]{3,2,1,0:T(4,128)(2,1)} %bitcast.47) | data formatting | bytes 8388608
  11.9 0.0 copy-start.2
  11.9 6.6 %copy.10 = bf16[1024,2048]{1,0:T(8,128)(2,1)} copy(bf16[1024,2048]{0,1:T(8,128)(2,1)} %bitcast.45) | data formatting | bytes 8388608 | tf_op jit(solution)/shard_map/dot_general | solution.py:145
  18.5 0.0 copy-done.2
  18.5 4.5 fusion.5
  23.0 0.0 reduce-scatter.6.cloned.1.call-update
  23.0 0.0 reduce-scatter.4.cloned.1.call-start
  23.1 0.0 copy-done
  23.1 6.8 %fusion.26 = f32[2048,1024]{1,0:T(8,128)} fusion(bf16[2048,512]{1,0:T(8,128)(2,1)S(1)} %copy-done, bf16[512,1024]{1,0:T(8,128)(2,1)} %param.11), kind=kOutput, calls=%fused_computation.47 | convolution fusion | flops 2147483648 | bytes 11534336 | tf_op jit(solution)/shard_map/dot_general | solution.py:132
  29.9 0.0 copy-start.3
  29.9 0.0 reduce-scatter.4.cloned.1.call-update
  29.9 0.0 all-gather.6.cloned.1.call-start
  30.0 0.5 copy-done.3
  30.6 0.1 fusion.21
  30.6 41.4 %reduce-scatter.6.cloned.1.call-done = f32[256,1,256]{2,0,1:T(8,128)} async-done(((f32[256,4,256]{2,0,1:T(8,128)}), f32[256,1,256]{2,0,1:T(8,128)}) %reduce-scatter.6.cloned.1.call-update) | async-done | bytes 262160 | tf_op jit(solution)/shard_map/reduce_scatter | solution.py:151
  72.0 0.9 fusion.15
  73.0 1.6 fusion.17
  74.5 0.8 pad_maximum_fusion.3
  75.3 0.0 all-gather.6.cloned.1.call-update
  75.3 0.0 all-gather.4.cloned.1.call-start
  75.4 0.8 dynamic_slice.3
  76.2 0.1 fusion.18
  76.3 0.3 multiply_cosine_fusion.1
  76.6 93.8 %reduce-scatter.4.cloned.1.call-done = f32[128,1024]{1,0:T(8,128)} async-done(((f32[2048,1024]{1,0:T(8,128)}), f32[128,1024]{1,0:T(8,128)}) %reduce-scatter.4.cloned.1.call-update) | async-done | bytes 524304 | tf_op jit(solution)/shard_map/reduce_scatter | solution.py:131
  170.4 1.1 copy.14
  171.5 0.3 subtract_convert_fusion
  171.8 0.1 pad_maximum_fusion.2
  172.0 0.7 pad_maximum_fusion.1
  172.7 0.0 all-gather.4.cloned.1.call-update
  172.7 80.0 %all-gather.6.cloned.1.call-done = bf16[4096,384]{1,0:T(8,128)(2,1)} async-done(((bf16[256,384]{1,0:T(8,128)(2,1)}), bf16[4096,384]{1,0:T(8,128)(2,1)}) %all-gather.6.cloned.1.call-update) | async-done | bytes 3145744 | tf_op jit(solution)/shard_map/all_gather | solution.py:157
  252.8 2.1 fusion.25
  254.8 1.5 concatenate.32.refs_3_
  256.3 1.5 pad_maximum_fusion.refs_2_
  257.9 29.1 %all-gather.4.cloned.1.call-done = bf16[512,1152]{1,0:T(8,128)(2,1)} async-done(((bf16[128,1152]{1,0:T(8,128)(2,1)}), bf16[512,1152]{1,0:T(8,128)(2,1)}) %all-gather.4.cloned.1.call-update) | async-done | bytes 1179664 | tf_op jit(solution)/shard_map/all_gather | solution.py:163
  287.0 0.0 copy-start.1
  287.0 1.4 slice.50.refs_0_
  288.5 0.9 slice.51.refs_1_
  289.4 0.0 copy-done.1
  289.4 54.1 %attention.1 = (bf16[512,1024]{1,0:T(8,128)(2,1)}, f32[512,128]{1,0:T(8,128)S(1)}) custom-call(bf16[512,1024]{1,0:T(8,128)(2,1)S(1)} %slice.50.refs_0_, bf16[512,128]{1,0:T(8,128)(2,1)S(1)} %slice.51.refs_1_, bf16[4096,256]{1,0:T(8,128)(2,1)S(1)} %copy-done.1, bf16[4096,256]{1,0:T(8,128)(2,1)} %concatenate.32.refs_3_), custom_call_target="tpu_custom_call" | custom-call | tf_op jit(solution)/shard_map/attention/pallas_call | solution.py:89
  343.4 0.1 copy.11
  343.5 7.5 %all_to_all.10 = f32[4,128,8]{1,2,0:T(8,128)S(1)} all-to-all(f32[4,128,8]{1,2,0:T(8,128)S(1)} %copy.11), channel_id=1, replica_groups=mesh['head'=4,'inner'=16,'outer'=4] {'outer'}, dimensions={0} | all-to-all | bytes 32768 | tf_op jit(solution)/shard_map/all_to_all | solution.py:169
  351.0 3.5 all-to-all-start
  354.6 0.2 all-gather.8.cloned.1.call-start
  354.8 0.1 copy.12
  355.0 1.9 mul.131
  356.9 2.7 mul.132
  359.6 5.8 %all-to-all-done = bf16[4,128,1024]{2,1,0:T(8,128)(2,1)S(1)} async-done(((bf16[4,128,1024]{2,1,0:T(8,128)(2,1)}), bf16[4,128,1024]{2,1,0:T(8,128)(2,1)S(1)}, u32[]{:S(2)}, u32[]{:S(2)}) %all-to-all-start) | async-done | bytes 1048608 | tf_op jit(solution)/shard_map/all_to_all | solution.py:166
  365.4 2.7 multiply_reduce_fusion
  368.1 0.0 all-gather.8.cloned.1.call-update
  368.1 0.0 reduce-scatter.8.cloned.1.call-start
  368.2 1.4 copy.20
  369.6 1.3 copy.13
  370.9 79.4 %all-gather.8.cloned.1.call-done = bf16[2048,1024]{1,0:T(8,128)(2,1)} async-done(((bf16[128,1024]{1,0:T(8,128)(2,1)}), bf16[2048,1024]{1,0:T(8,128)(2,1)}) %all-gather.8.cloned.1.call-update) | async-done | bytes 4194320 | tf_op jit(solution)/shard_map/all_gather | solution.py:180
  450.3 6.2 %fusion.2 = bf16[2048,4,128]{2,0,1:T(8,128)(2,1)} fusion(bf16[4,128,1024]{2,1,0:T(8,128)(2,1)} %bitcast.52, bf16[2048,1024]{1,0:T(8,128)(2,1)} %all-gather.8.cloned.1.call-done), kind=kOutput, calls=%fused_computation.2 | convolution fusion | flops 2148532224 | bytes 7340032 | tf_op jit(solution)/shard_map/dot_general | solution.py:179
  456.5 0.0 reduce-scatter.8.cloned.1.call-update
  456.5 65.0 %reduce-scatter.8.cloned.1.call-done = bf16[2048,1,128]{2,0,1:T(8,128)(2,1)} async-done(((bf16[2048,4,128]{2,0,1:T(8,128)(2,1)}), bf16[2048,1,128]{2,0,1:T(8,128)(2,1)}) %reduce-scatter.8.cloned.1.call-update) | async-done | bytes 524304 | tf_op jit(solution)/shard_map/reduce_scatter | solution.py:185
  (9 shorter events, 0.1 us)
Async XLA Ops:
  6.5 16.6 %copy-start = (bf16[2048,512]{1,0:T(8,128)(2,1)S(1)}, bf16[2048,512]{1,0:T(8,128)(2,1)}, u32[]{:S(2)}) copy-start(bf16[2048,512]{1,0:T(8,128)(2,1)} %param.7) | copy-start | bytes 6291460
  6.5 65.5 %reduce-scatter.6.cloned.1.call-start = ((), (), s32[]{:S(2)}) async-start(), calls=%async_computation.7 | async-start | bytes 1310720 | tf_op jit(solution)/shard_map/reduce_scatter | solution.py:151
  11.9 6.6 %copy-start.2 = (bf16[256,2048]{1,0:T(8,128)(2,1)S(1)}, bf16[256,2048]{1,0:T(8,128)(2,1)}, u32[]{:S(2)}) copy-start(bf16[256,2048]{1,0:T(8,128)(2,1)} %param.8) | copy-start | bytes 3145732
  23.0 147.3 %reduce-scatter.4.cloned.1.call-start = ((), (), s32[]{:S(2)}) async-start(), calls=%async_computation.5 | async-start | bytes 8912896 | tf_op jit(solution)/shard_map/reduce_scatter | solution.py:131
  29.9 0.7 copy-start.3
  29.9 222.8 %all-gather.6.cloned.1.call-start = ((), (), s32[]{:S(2)}) async-start(), calls=%async_computation.8 | async-start | bytes 3342336 | tf_op jit(solution)/shard_map/all_gather | solution.py:157
  75.3 211.7 %all-gather.4.cloned.1.call-start = ((), (), s32[]{:S(2)}) async-start(), calls=%async_computation.6 | async-start | bytes 1474560 | tf_op jit(solution)/shard_map/all_gather | solution.py:163
  287.0 2.4 copy-start.1
  351.0 14.4 %all-to-all-start = ((bf16[4,128,1024]{2,1,0:T(8,128)(2,1)}), bf16[4,128,1024]{2,1,0:T(8,128)(2,1)S(1)}, u32[]{:S(2)}, u32[]{:S(2)}) async-start(bf16[4,128,1024]{2,1,0:T(8,128)(2,1)} %bitcast.7), calls=%async_computation.2 | async-start | bytes 2097152 | tf_op jit(solution)/shard_map/all_to_all | solution.py:166
  354.6 95.7 %all-gather.8.cloned.1.call-start = ((), (), s32[]{:S(2)}) async-start(), calls=%async_computation.9 | async-start | bytes 4456448 | tf_op jit(solution)/shard_map/all_gather | solution.py:180
  368.1 153.4 %reduce-scatter.8.cloned.1.call-start = ((), (), s32[]{:S(2)}) async-start(), calls=%async_computation.10 | async-start | bytes 2621440 | tf_op jit(solution)/shard_map/reduce_scatter | solution.py:185
Sparse Core Ops, SparseCore 0:
  23.2 48.8 reduce-scatter.5
  74.6 95.7 reduce-scatter.3
  172.2 80.5 all-gather.5
  254.4 32.5 all-gather.3
  368.2 82.0 all-gather.7
  456.6 64.7 reduce-scatter.7
